TPU v7x, 32 devices: a whole 2x2x4 slice. The times are simulated.
32 devices in a mesh: shard: 2 (over x), tensor: 4 (over y, core), section: 4 (over z).
Axes of the slice: x: 2, y: 2, z: 4, core: 2. Of those that a mesh axis runs over, the one named last changes fastest.
Arguments:
- grad_kv: bfloat16 [16, 1024, 2048], P(('shard', 'section'), None, 'tensor'), may hold values from -65000 to 65000
- grad_gate: bfloat16 [16, 512, 2048], P(('shard', 'section'), None, 'tensor'), may hold values from -65000 to 65000
- grad_laurel: bfloat16 [16, 128, 2048], P(('shard', 'section'), None, 'tensor'), may hold values from -65000 to 65000
- master_kv: float32 [1024, 2048], P(('shard', 'section'), 'tensor'), may hold values from -0.1 to 0.1
- master_gate: float32 [512, 2048], P(('shard', 'section'), 'tensor'), may hold values from -0.1 to 0.1
- master_laurel: float32 [128, 2048], P(('shard', 'section'), 'tensor'), may hold values from -0.1 to 0.1
- moment_kv: float32 [1024, 2048], P(('shard', 'section'), 'tensor'), may hold values from -0.1 to 0.1
- moment_gate: float32 [512, 2048], P(('shard', 'section'), 'tensor'), may hold values from -0.1 to 0.1
- moment_laurel: float32 [128, 2048], P(('shard', 'section'), 'tensor'), may hold values from -0.1 to 0.1
- second_kv: float32 [1024, 2048], P(('shard', 'section'), 'tensor'), may hold values from 0.01 to 1
- second_gate: float32 [512, 2048], P(('shard', 'section'), 'tensor'), may hold values from 0.01 to 1
- second_laurel: float32 [128, 2048], P(('shard', 'section'), 'tensor'), may hold values from 0.01 to 1
Outputs:
- new_master_kv: float32 [1024, 2048], P(('shard', 'section'), 'tensor')
- new_master_gate: float32 [512, 2048], P(('shard', 'section'), 'tensor')
- new_master_laurel: float32 [128, 2048], P(('shard', 'section'), 'tensor')
- new_moment_kv: float32 [1024, 2048], P(('shard', 'section'), 'tensor')
- new_moment_gate: float32 [512, 2048], P(('shard', 'section'), 'tensor')
- new_moment_laurel: float32 [128, 2048], P(('shard', 'section'), 'tensor')
- new_second_kv: float32 [1024, 2048], P(('shard', 'section'), 'tensor')
- new_second_gate: float32 [512, 2048], P(('shard', 'section'), 'tensor')
- new_second_laurel: float32 [128, 2048], P(('shard', 'section'), 'tensor')
- weights_kv: bfloat16 [1024, 2048], P(None, 'tensor')
- weights_gate: bfloat16 [512, 2048], P(None, 'tensor')
- weights_laurel: bfloat16 [128, 2048], P(None, 'tensor')
All inputs are finite; a program needn't handle non-finite values.
Results may differ from a plain program's by a relative error of at most 0.015.
Values may be sent and summed in bfloat16 or wider, within the bound.
A program may use at most 64 MiB of HBM per device.

v0:
```python
import math

import jax
import jax.numpy as jnp
from jax import lax
from jax.sharding import PartitionSpec as P

STEP = 10


beta_one = 0.9
beta_two = 0.95
adam_eps = 1e-08
learn_rate = 0.05
weight_decay = 0.1
clip_rms = 0.5


def reduce_group(gradient):
    return lax.psum_scatter(
        jnp.sum(gradient, axis=0, dtype=jnp.float32),
        ("shard", "section"),
        scatter_dimension=0,
        tiled=True,
    )


def adamw_group(master, moment, second, summed, factor):
    clipped = factor * summed
    moment_new = beta_one * moment + (1.0 - beta_one) * clipped
    second_new = beta_two * second + (1.0 - beta_two) * clipped * clipped
    first_hat = moment_new / (1.0 - beta_one**STEP)
    second_hat = second_new / (1.0 - beta_two**STEP)
    master_new = master - learn_rate * (
        first_hat / (jnp.sqrt(second_hat) + adam_eps) + weight_decay * master
    )
    return (master_new, moment_new, second_new)


def on_device(
    grad_kv,
    grad_gate,
    grad_laurel,
    master_kv,
    master_gate,
    master_laurel,
    moment_kv,
    moment_gate,
    moment_laurel,
    second_kv,
    second_gate,
    second_laurel,
):
    reduced = []
    partial_squares = []
    entries = 0
    for gradient in (grad_kv, grad_gate, grad_laurel):
        entries += gradient.shape[1] * gradient.shape[2] * lax.axis_size("tensor")
        summed = reduce_group(gradient)
        reduced.append(summed)
        local_square = jnp.sum(summed * summed)
        partial_squares.append(local_square)
    squares = lax.psum(
        partial_squares[0] + partial_squares[1] + partial_squares[2], ("shard", "tensor", "section")
    )
    ceiling = clip_rms * math.sqrt(entries)
    factor = ceiling / jnp.maximum(jnp.sqrt(squares), ceiling)
    kv_out = adamw_group(master_kv, moment_kv, second_kv, reduced[0], factor)
    gate_out = adamw_group(master_gate, moment_gate, second_gate, reduced[1], factor)
    laurel_out = adamw_group(master_laurel, moment_laurel, second_laurel, reduced[2], factor)
    weights_kv, weights_gate, weights_laurel = (
        lax.all_gather(kv_out[0].astype(jnp.bfloat16), ("shard", "section"), axis=0, tiled=True),
        lax.all_gather(gate_out[0].astype(jnp.bfloat16), ("shard", "section"), axis=0, tiled=True),
        lax.all_gather(
            laurel_out[0].astype(jnp.bfloat16), ("shard", "section"), axis=0, tiled=True
        ),
    )
    return (
        kv_out[0],
        gate_out[0],
        laurel_out[0],
        kv_out[1],
        gate_out[1],
        laurel_out[1],
        kv_out[2],
        gate_out[2],
        laurel_out[2],
        weights_kv,
        weights_gate,
        weights_laurel,
    )


def solution(mesh):
    placed = (
        P(("shard", "section"), None, "tensor"),
        P(("shard", "section"), None, "tensor"),
        P(("shard", "section"), None, "tensor"),
        P(("shard", "section"), "tensor"),
        P(("shard", "section"), "tensor"),
        P(("shard", "section"), "tensor"),
        P(("shard", "section"), "tensor"),
        P(("shard", "section"), "tensor"),
        P(("shard", "section"), "tensor"),
        P(("shard", "section"), "tensor"),
        P(("shard", "section"), "tensor"),
        P(("shard", "section"), "tensor"),
    )
    return jax.shard_map(
        on_device,
        mesh=mesh,
        in_specs=placed,
        out_specs=(
            P(("shard", "section"), "tensor"),
            P(("shard", "section"), "tensor"),
            P(("shard", "section"), "tensor"),
            P(("shard", "section"), "tensor"),
            P(("shard", "section"), "tensor"),
            P(("shard", "section"), "tensor"),
            P(("shard", "section"), "tensor"),
            P(("shard", "section"), "tensor"),
            P(("shard", "section"), "tensor"),
            P(None, "tensor"),
            P(None, "tensor"),
            P(None, "tensor"),
        ),
        check_vma=False,
    )
```

profile of v0, /device:TPU:0, one launch (start us, length us, event | category | flops | bytes accessed | tf_op | source)
XLA Modules:
  0.0 336.1 jit_solution(13623160437189734520)
XLA Ops:
  7.2 0.0 copy-start
  7.2 0.0 reduce-scatter.8.cloned.1.call-start
  7.2 1.8 convert_reduce_fusion.2
  9.1 0.0 reduce-scatter.8.cloned.1.call-update
  9.1 0.0 reduce-scatter.6.cloned.1.call-start
  9.2 2.5 convert_reduce_fusion.1
  11.6 0.0 reduce-scatter.6.cloned.1.call-update
  11.7 0.0 reduce-scatter.4.cloned.1.call-start
  11.7 1.7 convert_reduce_fusion
  13.5 0.0 copy-start.7
  13.5 0.0 reduce-scatter.4.cloned.1.call-update
  13.5 0.0 copy-start.9
  13.5 0.0 copy-start.10
  13.5 0.0 copy-start.11
  13.5 0.0 all-gather.2.cloned.1.call-start
  13.6 62.3 %reduce-scatter.8.cloned.1.call-done = f32[16,512]{1,0:T(8,128)} async-done(((f32[128,512]{1,0:T(8,128)}), f32[16,512]{1,0:T(8,128)}) %reduce-scatter.8.cloned.1.call-update) | async-done | bytes 32784 | tf_op jit(solution)/shard_map/reduce_scatter | solution.py:20
  75.9 1.4 multiply_reduce_fusion.2
  77.3 64.8 %reduce-scatter.6.cloned.1.call-done = f32[64,512]{1,0:T(8,128)} async-done(((f32[512,512]{1,0:T(8,128)}), f32[64,512]{1,0:T(8,128)}) %reduce-scatter.6.cloned.1.call-update) | async-done | bytes 131088 | tf_op jit(solution)/shard_map/reduce_scatter | solution.py:20
  142.1 1.6 multiply_reduce_fusion.1
  143.8 69.6 %reduce-scatter.4.cloned.1.call-done = f32[128,512]{1,0:T(8,128)} async-done(((f32[1024,512]{1,0:T(8,128)}), f32[128,512]{1,0:T(8,128)}) %reduce-scatter.4.cloned.1.call-update) | async-done | bytes 262160 | tf_op jit(solution)/shard_map/reduce_scatter | solution.py:20
  213.4 1.6 multiply_reduce_fusion
  217.0 39.6 %psum.7 = f32[]{:T(128)} all-reduce(f32[]{:T(128)S(6)} %add.60), channel_id=1, replica_groups=mesh['shard'=2,'tensor'=4,'section'=4] {'shard','tensor','section'}, use_global_device_ids=true, to_apply=%region_9.0 | all-reduce | flops 1 | bytes 8 | tf_op jit(solution)/shard_map/psum | solution.py:63
  257.3 2.0 fusion.7
  259.3 0.0 all-gather.2.cloned.1.call-update
  259.4 0.8 fusion.5
  260.2 34.2 %all_gather.10 = bf16[512,512]{1,0:T(8,128)(2,1)S(1)} all-gather(bf16[64,512]{1,0:T(8,128)(2,1)S(1)} %get-tuple-element.16), channel_id=1, replica_groups=mesh['shard'=2,'tensor'=4,'section'=4] {'shard','section'}, dimensions={0}, use_global_device_ids=true | all-gather | bytes 589824 | tf_op jit(solution)/shard_map/all_gather | solution.py:73
  294.4 0.0 copy-done.9
  294.4 0.7 fusion.3
  295.1 30.7 %all_gather.11 = bf16[128,512]{1,0:T(8,128)(2,1)S(1)} all-gather(bf16[16,512]{1,0:T(8,128)(2,1)S(1)} %get-tuple-element.12), channel_id=1, replica_groups=mesh['shard'=2,'tensor'=4,'section'=4] {'shard','section'}, dimensions={0}, use_global_device_ids=true | all-gather | bytes 147456 | tf_op jit(solution)/shard_map/all_gather | solution.py:74
  325.8 2.3 copy.27
  328.1 0.8 copy.28
  328.9 0.7 copy.29
  (19 shorter events, 0.0 us)
Async XLA Ops:
  7.2 4.5 %copy-start = (bf16[2,1024,512]{2,1,0:T(8,128)(2,1)S(1)}, bf16[2,1024,512]{2,1,0:T(8,128)(2,1)}, u32[]{:S(2)}) copy-start(bf16[2,1024,512]{2,1,0:T(8,128)(2,1)} %param.12) | copy-start | bytes 6291460
  7.2 68.7 %reduce-scatter.8.cloned.1.call-start = ((), (), s32[]{:S(2)}) async-start(), calls=%async_computation.5 | async-start | bytes 294912 | tf_op jit(solution)/shard_map/reduce_scatter | solution.py:20
  9.1 133.0 %reduce-scatter.6.cloned.1.call-start = ((), (), s32[]{:S(2)}) async-start(), calls=%async_computation.4 | async-start | bytes 1179648 | tf_op jit(solution)/shard_map/reduce_scatter | solution.py:20
  11.7 201.7 %reduce-scatter.4.cloned.1.call-start = ((), (), s32[]{:S(2)}) async-start(), calls=%async_computation.3 | async-start | bytes 2359296 | tf_op jit(solution)/shard_map/reduce_scatter | solution.py:20
  13.5 243.8 %copy-start.2 = (f32[128,512]{1,0:T(8,128)S(1)}, f32[128,512]{1,0:T(8,128)}, u32[]{:S(2)}) copy-start(f32[128,512]{1,0:T(8,128)} %param.15) | copy-start | bytes 786436
  13.5 243.8 %copy-start.3 = (f32[128,512]{1,0:T(8,128)S(1)}, f32[128,512]{1,0:T(8,128)}, u32[]{:S(2)}) copy-start(f32[128,512]{1,0:T(8,128)} %param.18) | copy-start | bytes 786436
  13.5 243.8 %copy-start.4 = (f32[128,512]{1,0:T(8,128)S(1)}, f32[128,512]{1,0:T(8,128)}, u32[]{:S(2)}) copy-start(f32[128,512]{1,0:T(8,128)} %param.21) | copy-start | bytes 786436
  13.5 245.9 %copy-start.5 = (f32[64,512]{1,0:T(8,128)S(1)}, f32[64,512]{1,0:T(8,128)}, u32[]{:S(2)}) copy-start(f32[64,512]{1,0:T(8,128)} %param.16) | copy-start | bytes 393220
  13.5 245.9 %copy-start.6 = (f32[64,512]{1,0:T(8,128)S(1)}, f32[64,512]{1,0:T(8,128)}, u32[]{:S(2)}) copy-start(f32[64,512]{1,0:T(8,128)} %param.19) | copy-start | bytes 393220
  13.5 245.9 %copy-start.7 = (f32[64,512]{1,0:T(8,128)S(1)}, f32[64,512]{1,0:T(8,128)}, u32[]{:S(2)}) copy-start(f32[64,512]{1,0:T(8,128)} %param.22) | copy-start | bytes 393220
  13.5 280.9 %copy-start.9 = (f32[16,512]{1,0:T(8,128)S(1)}, f32[16,512]{1,0:T(8,128)}, u32[]{:S(2)}) copy-start(f32[16,512]{1,0:T(8,128)} %param.17) | copy-start | bytes 98308
  13.5 280.9 %copy-start.10 = (f32[16,512]{1,0:T(8,128)S(1)}, f32[16,512]{1,0:T(8,128)}, u32[]{:S(2)}) copy-start(f32[16,512]{1,0:T(8,128)} %param.20) | copy-start | bytes 98308
  13.5 280.9 %copy-start.11 = (f32[16,512]{1,0:T(8,128)S(1)}, f32[16,512]{1,0:T(8,128)}, u32[]{:S(2)}) copy-start(f32[16,512]{1,0:T(8,128)} %param.23) | copy-start | bytes 98308
  13.5 312.3 %all-gather.2.cloned.1.call-start = ((), (), s32[]{:S(2)}) async-start(), calls=%async_computation.6 | async-start | bytes 1179648 | tf_op jit(solution)/shard_map/all_gather | solution.py:72
  75.9 218.6 %copy-start.8 = (f32[16,512]{1,0:T(8,128)S(1)}, f32[16,512]{1,0:T(8,128)}, u32[]{:S(2)}) copy-start(f32[16,512]{1,0:T(8,128)} %reduce-scatter.8.cloned.1.call-done) | copy-start | bytes 98308
  142.1 117.2 %copy-start.1 = (f32[64,512]{1,0:T(8,128)S(1)}, f32[64,512]{1,0:T(8,128)}, u32[]{:S(2)}) copy-start(f32[64,512]{1,0:T(8,128)} %reduce-scatter.6.cloned.1.call-done) | copy-start | bytes 393220
Sparse Core Ops, SparseCore 0:
  11.9 63.8 reduce-scatter.7
  79.8 62.2 reduce-scatter.5
  146.1 67.2 reduce-scatter.3
  259.5 41.6 all-gather.1
where the time goes:
time: 337 us; the launch traced here: 336 us
  waiting for transfers between devices  197 us (58%)
  blocking collectives  105 us (31%)
  between operations  16.6 us (5%)
  other arithmetic  14.2 us (4%)
  local copies, waits for them, and re-layouts  3.77 us (1%)
    reduce_scatter x3, waiting for transfers between devices, reduce_group(): lax.psum_scatter(jnp.sum(gradient, axis=0, dtype=jnp.float32), ('shard',...  197 us
    psum x1, blocking collectives, on_device(): lax.psum(partial_squares[0] + partial_squares[1] + partial_squares[2], ('...  39.6 us
    all_gather x1, blocking collectives, on_device(): lax.all_gather(gate_out[0].astype(jnp.bfloat16), ('shard', 'section'), ax...  34.2 us
    all_gather x1, blocking collectives, on_device(): lax.all_gather(laurel_out[0].astype(jnp.bfloat16), ('shard', 'section'),...  30.7 us
  transfers between devices with their start and end apart: 4, of which 3 were waited for; matrix products, arithmetic and copies ran while one was open for 3% of the time, Pallas kernels for 0%

commit v1 on v0

v1 whole, which is shorter than its diff:
```python
import functools
import math

import jax
import jax.numpy as jnp
from jax import lax
from jax.experimental import pallas as pl
from jax.experimental.pallas import tpu as pltpu
from jax.sharding import PartitionSpec as P

STEP = 10

beta_one = 0.9
beta_two = 0.95
adam_eps = 1e-08
learn_rate = 0.05
weight_decay = 0.1
clip_rms = 0.5

WIRE = jnp.bfloat16
MESH = pl.DeviceIdType.MESH


def adamw_group(master, moment, second, summed, factor):
    clipped = factor * summed
    moment_new = beta_one * moment + (1.0 - beta_one) * clipped
    second_new = beta_two * second + (1.0 - beta_two) * clipped * clipped
    first_hat = moment_new / (1.0 - beta_one**STEP)
    second_hat = second_new / (1.0 - beta_two**STEP)
    master_new = master - learn_rate * (
        first_hat / (jnp.sqrt(second_hat) + adam_eps) + weight_decay * master
    )
    return (master_new, moment_new, second_new)


def section_order(count):
    return sorted(range(1, count), key=lambda k: (abs(k - count // 2), -k)) + [0]


def kernel(sizes, rows, batches, ceiling, *refs):
    shards, sections, tensors = sizes
    grads, states = refs[0:3], refs[3:12]
    new_states, weights = refs[12:21], refs[21]
    grad_buf, state_buf, new_buf = refs[22:25], refs[25:34], refs[34:43]
    (
        x_out, x_in, z_out, z_in, total, own_weights,
        norm_out, group_in, tensor_out, tensor_in,
        load_sem, state_sem, store_sem, own_sem,
        x_send, x_recv, z_send, z_recv,
        group_send, group_recv, tensor_send, tensor_recv,
        gz_send, gz_recv, gx_send, gx_recv,
    ) = refs[43:]
    s, t, z = lax.axis_index("shard"), lax.axis_index("tensor"), lax.axis_index("section")
    order = section_order(sections)
    starts = [sum(rows[:g]) for g in range(3)]

    def shard_at(j):
        return lax.rem(s + j, shards)

    def section_at(k):
        return lax.rem(z + k, sections)

    group = [(a, b) for a in range(shards) for b in range(sections) if (a, b) != (0, 0)]

    barrier = pltpu.get_barrier_semaphore()
    for a, b in group:
        pl.semaphore_signal(
            barrier, inc=1, device_id={"shard": shard_at(a), "section": section_at(b)}, device_id_type=MESH
        )
    for c in range(1, tensors):
        pl.semaphore_signal(barrier, inc=1, device_id={"tensor": lax.rem(t + c, tensors)}, device_id_type=MESH)

    loads = {}
    for j in list(range(1, shards)) + [0]:
        for g in range(3):
            copy = pltpu.make_async_copy(
                grads[g].at[:, shard_at(j)], grad_buf[g].at[:, shard_at(j)], load_sem.at[j, g]
            )
            copy.start()
            loads[j, g] = copy
    state_loads = []
    for i in range(9):
        copy = pltpu.make_async_copy(states[i], state_buf[i], state_sem.at[i])
        copy.start()
        state_loads.append(copy)

    def partial(g, shard, section):
        value = grad_buf[g][0, shard, section].astype(jnp.float32)
        for m in range(1, batches):
            value = value + grad_buf[g][m, shard, section].astype(jnp.float32)
        return value

    sends = []
    x_copies = {}
    waited = set()
    for k in order:
        for j in range(1, shards):
            for g in range(3):
                if (j, g) not in waited:
                    loads[j, g].wait()
                    waited.add((j, g))
                x_out[j - 1, k, starts[g] : starts[g] + rows[g]] = partial(
                    g, shard_at(j), section_at(k)
                ).astype(WIRE)
        if k == order[0]:
            pl.semaphore_wait(barrier, len(group) + tensors - 1)
        for j in range(1, shards):
            copy = pltpu.make_async_remote_copy(
                src_ref=x_out.at[j - 1, k],
                dst_ref=x_in.at[j - 1, k],
                send_sem=x_send.at[j - 1, k],
                recv_sem=x_recv.at[j - 1, k],
                device_id={"shard": shard_at(j)},
                device_id_type=MESH,
            )
            copy.start()
            x_copies[j, k] = copy
            sends.append(copy)

    for g in range(3):
        loads[0, g].wait()
    z_copies = {}
    for k in order:
        for j in range(1, shards):
            x_copies[j, k].wait_recv()
        for g in range(3):
            span = slice(starts[g], starts[g] + rows[g])
            value = partial(g, s, section_at(k))
            for j in range(1, shards):
                value = value + x_in[j - 1, k, span].astype(jnp.float32)
            if k:
                z_out[k - 1, span] = value.astype(WIRE)
            else:
                total[span] = value
        if k:
            copy = pltpu.make_async_remote_copy(
                src_ref=z_out.at[k - 1],
                dst_ref=z_in.at[k - 1],
                send_sem=z_send.at[k - 1],
                recv_sem=z_recv.at[k - 1],
                device_id={"section": section_at(k)},
                device_id_type=MESH,
            )
            copy.start()
            z_copies[k] = copy
            sends.append(copy)
    for k in order[:-1]:
        z_copies[k].wait_recv()
    summed = total[...]
    for k in order[:-1]:
        summed = summed + z_in[k - 1].astype(jnp.float32)
    total[...] = summed

    def fold(value):
        width = value.shape[1]
        return sum(value[:, c : c + 128] for c in range(0, width, 128))

    squares = fold(jnp.sum(summed * summed, axis=0, keepdims=True))
    norm_out[...] = jnp.broadcast_to(squares, norm_out.shape)
    group_copies = []
    for i, (a, b) in enumerate(group):
        copy = pltpu.make_async_remote_copy(
            src_ref=norm_out,
            dst_ref=group_in.at[i],
            send_sem=group_send.at[i],
            recv_sem=group_recv.at[i],
            device_id={"shard": shard_at(a), "section": section_at(b)},
            device_id_type=MESH,
        )
        copy.start()
        group_copies.append(copy)
        sends.append(copy)
    for copy in state_loads:
        copy.wait()
    value = norm_out[...]
    for i, copy in enumerate(group_copies):
        copy.wait_recv()
        value = value + group_in[i]
    tensor_out[...] = value
    tensor_copies = []
    for c in range(1, tensors):
        copy = pltpu.make_async_remote_copy(
            src_ref=tensor_out,
            dst_ref=tensor_in.at[c - 1],
            send_sem=tensor_send.at[c - 1],
            recv_sem=tensor_recv.at[c - 1],
            device_id={"tensor": lax.rem(t + c, tensors)},
            device_id_type=MESH,
        )
        copy.start()
        tensor_copies.append(copy)
        sends.append(copy)
    for i, copy in enumerate(tensor_copies):
        copy.wait_recv()
        value = value + tensor_in[i]
    norm = jnp.sqrt(jnp.sum(value[0:1], axis=1, keepdims=True))
    factor = ceiling / jnp.maximum(norm, ceiling)

    for g in range(3):
        span = slice(starts[g], starts[g] + rows[g])
        new = adamw_group(
            state_buf[g][...], state_buf[3 + g][...], state_buf[6 + g][...], total[span], factor
        )
        own_weights[span] = new[0].astype(jnp.bfloat16)
        for i in range(3):
            new_buf[3 * i + g][...] = new[i]

    gx_copies = {}

    def forward(k, source):
        for j in range(1, shards):
            copy = pltpu.make_async_remote_copy(
                src_ref=source,
                dst_ref=weights.at[s, lax.rem(z - k + sections, sections)],
                send_sem=gx_send.at[j - 1, k],
                recv_sem=gx_recv.at[j - 1, k],
                device_id={"shard": shard_at(j)},
                device_id_type=MESH,
            )
            copy.start()
            gx_copies[j, k] = copy
            sends.append(copy)

    forward(0, own_weights)
    gz_copies = {}
    for k in order[:-1]:
        copy = pltpu.make_async_remote_copy(
            src_ref=own_weights,
            dst_ref=weights.at[s, z],
            send_sem=gz_send.at[k - 1],
            recv_sem=gz_recv.at[k - 1],
            device_id={"section": section_at(k)},
            device_id_type=MESH,
        )
        copy.start()
        gz_copies[k] = copy
        sends.append(copy)
    own = pltpu.make_async_copy(own_weights, weights.at[s, z], own_sem)
    own.start()
    stores = []
    for i in range(9):
        copy = pltpu.make_async_copy(new_buf[i], new_states[i], store_sem.at[i])
        copy.start()
        stores.append(copy)
    for k in reversed(order[:-1]):
        gz_copies[k].wait_recv()
        forward(k, weights.at[s, lax.rem(z - k + sections, sections)])
    own.wait()
    for copy in stores:
        copy.wait()
    for copy in gx_copies.values():
        copy.wait_recv()
    for copy in sends:
        copy.wait_send()


def on_device(*arguments):
    shards, sections, tensors = (lax.axis_size(a) for a in ("shard", "section", "tensor"))
    grads, states = arguments[:3], arguments[3:]
    batches, _, width = grads[0].shape
    rows = [states[g].shape[0] for g in range(3)]
    height = sum(rows)
    entries = sum(gradient.shape[1] * width * tensors for gradient in grads)
    ceiling = clip_rms * math.sqrt(entries)
    grads = [
        gradient.reshape(batches, shards, sections, rows[g], width) for g, gradient in enumerate(grads)
    ]
    n_group = shards * sections - 1
    dma = pltpu.SemaphoreType.DMA
    scratch = (
        [pltpu.VMEM(gradient.shape, jnp.bfloat16) for gradient in grads]
        + [pltpu.VMEM(state.shape, jnp.float32) for state in states]
        + [pltpu.VMEM(state.shape, jnp.float32) for state in states]
        + [
            pltpu.VMEM((shards - 1, sections, height, width), WIRE),
            pltpu.VMEM((shards - 1, sections, height, width), WIRE),
            pltpu.VMEM((sections - 1, height, width), WIRE),
            pltpu.VMEM((sections - 1, height, width), WIRE),
            pltpu.VMEM((height, width), jnp.float32),
            pltpu.VMEM((height, width), jnp.bfloat16),
            pltpu.VMEM((8, 128), jnp.float32),
            pltpu.VMEM((n_group, 8, 128), jnp.float32),
            pltpu.VMEM((8, 128), jnp.float32),
            pltpu.VMEM((tensors - 1, 8, 128), jnp.float32),
            dma((shards, 3)),
            dma((9,)),
            dma((9,)),
            dma,
            dma((shards - 1, sections)),
            dma((shards - 1, sections)),
            dma((sections - 1,)),
            dma((sections - 1,)),
            dma((n_group,)),
            dma((n_group,)),
            dma((tensors - 1,)),
            dma((tensors - 1,)),
            dma((sections - 1,)),
            dma((sections - 1,)),
            dma((shards - 1, sections)),
            dma((shards - 1, sections)),
        ]
    )
    results = pl.pallas_call(
        functools.partial(kernel, (shards, sections, tensors), rows, batches, ceiling),
        out_shape=[jax.ShapeDtypeStruct(state.shape, jnp.float32) for state in states]
        + [jax.ShapeDtypeStruct((shards, sections, height, width), jnp.bfloat16)],
        in_specs=[pl.BlockSpec(memory_space=pl.ANY)] * 12,
        out_specs=[pl.BlockSpec(memory_space=pl.ANY)] * 10,
        scratch_shapes=scratch,
        compiler_params=pltpu.CompilerParams(
            collective_id=0, has_side_effects=True, vmem_limit_bytes=48 * 1024 * 1024
        ),
    )(*grads, *states)
    weights = []
    for g in range(3):
        start = sum(rows[:g])
        part = lax.slice_in_dim(results[9], start, start + rows[g], axis=2)
        weights.append(part.reshape(shards * sections * rows[g], width))
    return (*results[:9], *weights)


def solution(mesh):
    grad = P(("shard", "section"), None, "tensor")
    state = P(("shard", "section"), "tensor")
    return jax.shard_map(
        on_device,
        mesh=mesh,
        in_specs=(grad,) * 3 + (state,) * 9,
        out_specs=(state,) * 9 + (P(None, "tensor"),) * 3,
        check_vma=False,
    )
```

time: 337 us -> 91.6 us (0.27)
  the two profiles are of different devices: /device:TPU:0 before, /device:TPU:16 now
where the time goes in v1:
time: 91.6 us; the launch traced here: 91 us
  Pallas kernels  71.8 us (78%)
  local copies, waits for them, and re-layouts  18.5 us (20%)
    pallas_call x1, Pallas kernels, on_device(): pl.pallas_call(functools.partial(kernel, (shards, sections, tensors), row...  71.8 us
    unnamed x31, local copies, waits for them, and re-layouts  15.9 us
    slice x3, local copies, waits for them, and re-layouts, on_device(): part = lax.slice_in_dim(results[9], start, start + rows[g], axis=2)  2.56 us

profile of v1, /device:TPU:16, one launch (start us, length us, event | category | flops | bytes accessed | tf_op | source)
XLA Modules:
  0.0 91.0 jit_solution(4529552596957121424)
XLA Ops:
  0.6 0.0 copy-start
  0.7 1.2 %copy-done = bf16[2,512,512]{2,1,0:T(8,128)(2,1)S(1)} copy-done((bf16[2,512,512]{2,1,0:T(8,128)(2,1)S(1)}, bf16[2,512,512]{2,1,0:T(8,128)(2,1)}, u32[]{:S(2)}) %copy-start) | copy-done | bytes 1048600
  1.9 0.0 copy-start.1
  1.9 0.9 %copy-done.1 = bf16[2,128,512]{2,1,0:T(8,128)(2,1)S(1)} copy-done((bf16[2,128,512]{2,1,0:T(8,128)(2,1)S(1)}, bf16[2,128,512]{2,1,0:T(8,128)(2,1)}, u32[]{:S(2)}) %copy-start.1) | copy-done | bytes 262168
  2.8 0.0 copy-start.2
  2.8 0.9 %copy-done.2 = f32[128,512]{1,0:T(8,128)S(1)} copy-done((f32[128,512]{1,0:T(8,128)S(1)}, f32[128,512]{1,0:T(8,128)}, u32[]{:S(2)}) %copy-start.2) | copy-done | bytes 262168
  3.8 0.0 copy-start.3
  3.8 0.9 %copy-done.3 = f32[128,512]{1,0:T(8,128)S(1)} copy-done((f32[128,512]{1,0:T(8,128)S(1)}, f32[128,512]{1,0:T(8,128)}, u32[]{:S(2)}) %copy-start.3) | copy-done | bytes 262168
  4.7 0.0 copy-start.4
  4.7 0.9 %copy-done.4 = f32[128,512]{1,0:T(8,128)S(1)} copy-done((f32[128,512]{1,0:T(8,128)S(1)}, f32[128,512]{1,0:T(8,128)}, u32[]{:S(2)}) %copy-start.4) | copy-done | bytes 262168
  5.7 0.0 copy-start.5
  5.7 0.9 copy-done.5
  6.6 0.0 copy-start.6
  6.6 0.9 copy-done.6
  7.5 0.0 copy-start.7
  7.5 0.9 copy-done.7
  8.4 0.8 copy-done.8
  9.2 0.8 copy-done.9
  9.9 0.8 copy-done.10
  10.7 71.8 %shard_map.211 = (f32[128,512]{1,0:T(8,128)S(1)}, f32[64,512]{1,0:T(8,128)S(1)}, f32[16,512]{1,0:T(8,128)S(1)}, f32[128,512]{1,0:T(8,128)S(1)}, f32[64,512]{1,0:...) custom-call(bf16[2,2,4,128,512]{4,3,2,1,0:T(8,128)(2,1)} %bitcast.8,, ...), custom_call_target="tpu_custom_call" | custom-call | tf_op jit(solution)/shard_map/pallas_call | solution.py:303
  82.5 0.7 slice.11
  83.2 0.8 slice.10
  84.0 1.1 %slice.9 = bf16[2,4,128,512]{3,2,1,0:T(8,128)(2,1)} slice(bf16[2,4,208,512]{3,2,1,0:T(8,128)(2,1)S(1)} %get-tuple-element.31), slice={[0:2], [0:4], [0:128], [0:512]} | slice | bytes 2097152 | tf_op jit(solution)/shard_map/slice | solution.py:317
  85.1 0.7 copy.33
  85.8 0.7 copy.34
  86.4 0.6 copy.35
  87.1 0.7 copy.36
  87.8 0.7 copy.37
  88.4 0.6 copy.38
  89.0 0.7 copy.39
  89.7 0.7 copy.40
  90.4 0.6 copy.41
  (3 shorter events, 0.0 us)
Async XLA Ops:
  0.6 1.2 %copy-start = (bf16[2,512,512]{2,1,0:T(8,128)(2,1)S(1)}, bf16[2,512,512]{2,1,0:T(8,128)(2,1)}, u32[]{:S(2)}) copy-start(bf16[2,512,512]{2,1,0:T(8,128)(2,1)} %param.13) | copy-start | bytes 3145732
  1.9 0.9 %copy-start.1 = (bf16[2,128,512]{2,1,0:T(8,128)(2,1)S(1)}, bf16[2,128,512]{2,1,0:T(8,128)(2,1)}, u32[]{:S(2)}) copy-start(bf16[2,128,512]{2,1,0:T(8,128)(2,1)} %param.14) | copy-start | bytes 786436
  2.8 0.9 %copy-start.2 = (f32[128,512]{1,0:T(8,128)S(1)}, f32[128,512]{1,0:T(8,128)}, u32[]{:S(2)}) copy-start(f32[128,512]{1,0:T(8,128)} %refs_3_.1) | copy-start | bytes 786436
  3.8 0.9 %copy-start.3 = (f32[128,512]{1,0:T(8,128)S(1)}, f32[128,512]{1,0:T(8,128)}, u32[]{:S(2)}) copy-start(f32[128,512]{1,0:T(8,128)} %refs_6_.1) | copy-start | bytes 786436
  4.7 0.9 %copy-start.4 = (f32[128,512]{1,0:T(8,128)S(1)}, f32[128,512]{1,0:T(8,128)}, u32[]{:S(2)}) copy-start(f32[128,512]{1,0:T(8,128)} %refs_9_.1) | copy-start | bytes 786436
  5.7 0.9 copy-start.5
  6.6 0.9 copy-start.6
  7.5 0.9 copy-start.7
  8.4 0.8 copy-start.8
  9.1 0.8 copy-start.9
  9.9 0.8 copy-start.10

commit v2 on v1

--- a/solution.py
+++ b/solution.py
@@ -18,6 +18,7 @@
 clip_rms = 0.5
 
 WIRE = jnp.bfloat16
+VMEM_LIMIT = 56 * 1024 * 1024
 MESH = pl.DeviceIdType.MESH
 
 
@@ -252,6 +253,22 @@
         copy.wait_recv()
     for copy in sends:
         copy.wait_send()
+
+
+def finish(rows, *refs):
+    sources, targets, sem = refs[:10], refs[10:22], refs[22]
+    copies = []
+    for g in range(3):
+        start = sum(rows[:g])
+        copies.append((sources[9].at[:, :, start : start + rows[g]], targets[9 + g]))
+    copies += list(zip(sources[:9], targets[:9]))
+    copies = [
+        pltpu.make_async_copy(source, target, sem.at[i]) for i, (source, target) in enumerate(copies)
+    ]
+    for copy in copies:
+        copy.start()
+    for copy in copies:
+        copy.wait()
 
 
 def on_device(*arguments):
@@ -302,21 +319,28 @@
     )
     results = pl.pallas_call(
         functools.partial(kernel, (shards, sections, tensors), rows, batches, ceiling),
-        out_shape=[jax.ShapeDtypeStruct(state.shape, jnp.float32) for state in states]
-        + [jax.ShapeDtypeStruct((shards, sections, height, width), jnp.bfloat16)],
-        in_specs=[pl.BlockSpec(memory_space=pl.ANY)] * 12,
-        out_specs=[pl.BlockSpec(memory_space=pl.ANY)] * 10,
+        out_shape=[pltpu.VMEM(state.shape, jnp.float32) for state in states]
+        + [pltpu.VMEM((shards, sections, height, width), jnp.bfloat16)],
+        in_specs=[pl.BlockSpec(memory_space=pltpu.HBM)] * 12,
+        out_specs=[pl.BlockSpec(memory_space=pltpu.VMEM)] * 10,
         scratch_shapes=scratch,
         compiler_params=pltpu.CompilerParams(
-            collective_id=0, has_side_effects=True, vmem_limit_bytes=48 * 1024 * 1024
+            collective_id=0, has_side_effects=True, vmem_limit_bytes=VMEM_LIMIT
         ),
     )(*grads, *states)
-    weights = []
-    for g in range(3):
-        start = sum(rows[:g])
-        part = lax.slice_in_dim(results[9], start, start + rows[g], axis=2)
-        weights.append(part.reshape(shards * sections * rows[g], width))
-    return (*results[:9], *weights)
+    full = [
+        jax.ShapeDtypeStruct((shards, sections, rows[g], width), jnp.bfloat16) for g in range(3)
+    ]
+    finished = pl.pallas_call(
+        functools.partial(finish, rows),
+        out_shape=[jax.ShapeDtypeStruct(state.shape, jnp.float32) for state in states] + full,
+        in_specs=[pl.BlockSpec(memory_space=pl.ANY)] * 10,
+        out_specs=[pl.BlockSpec(memory_space=pltpu.HBM)] * 12,
+        scratch_shapes=[dma((12,))],
+        compiler_params=pltpu.CompilerParams(vmem_limit_bytes=4 * 1024 * 1024),
+    )(*results)
+    weights = [part.reshape(-1, width) for part in finished[9:]]
+    return (*finished[:9], *weights)
 
 
 def solution(mesh):

time: 91.6 us -> 74.4 us (0.81)
  the two profiles are of different devices: /device:TPU:16 before, /device:TPU:0 now
where the time goes in v2:
time: 74.4 us; the launch traced here: 73.1 us
  Pallas kernels  72.4 us (97%)
    pallas_call x1, Pallas kernels, on_device(): pl.pallas_call(functools.partial(kernel, (shards, sections, tensors), row...  70.7 us
    pallas_call x1, Pallas kernels, on_device(): pl.pallas_call(functools.partial(finish, rows), out_shape=[jax.ShapeDtype...  1.7 us

profile of v2, /device:TPU:0, one launch (start us, length us, event | category | flops | bytes accessed | tf_op | source)
XLA Modules:
  0.0 73.1 jit_solution(10419781837737557006)
XLA Ops:
  0.6 70.7 %shard_map.211 = (f32[128,512]{1,0:T(8,128)S(1)}, f32[64,512]{1,0:T(8,128)S(1)}, f32[16,512]{1,0:T(8,128)S(1)}, f32[128,512]{1,0:T(8,128)S(1)}, f32[64,512]{1,0:...) custom-call(bf16[2,2,4,128,512]{4,3,2,1,0:T(8,128)(2,1)} %bitcast.6,, ...), custom_call_target="tpu_custom_call" | custom-call | tf_op jit(solution)/shard_map/pallas_call | solution.py:320
  71.4 1.7 %shard_map.212 = (f32[128,512]{1,0:T(8,128)}, f32[64,512]{1,0:T(8,128)}, f32[16,512]{1,0:T(8,128)}, f32[128,512]{1,0:T(8,128)}, f32[64,512]{1,0:T(8,128)}, /*ind...) custom-call(f32[128,512]{1,0:T(8,128)S(1)} %get-tuple-element.34.ref, ...), custom_call_target="tpu_custom_call" | custom-call | tf_op jit(solution)/shard_map/pallas_call | solution.py:334

commit v3 on v2

--- a/solution.py
+++ b/solution.py
@@ -19,6 +19,8 @@
 
 WIRE = jnp.bfloat16
 VMEM_LIMIT = 56 * 1024 * 1024
+PIECES = 4
+DEPTH = 2
 MESH = pl.DeviceIdType.MESH
 
 
@@ -206,36 +208,45 @@
         for i in range(3):
             new_buf[3 * i + g][...] = new[i]
 
+    width = own_weights.shape[1] // PIECES
     gx_copies = {}
-
-    def forward(k, source):
+    gz_copies = {}
+
+    def piece(ref, c):
+        return ref.at[:, c * width : (c + 1) * width]
+
+    def forward(k, c):
+        place = weights.at[s, lax.rem(z - k + sections, sections)]
         for j in range(1, shards):
             copy = pltpu.make_async_remote_copy(
-                src_ref=source,
-                dst_ref=weights.at[s, lax.rem(z - k + sections, sections)],
-                send_sem=gx_send.at[j - 1, k],
-                recv_sem=gx_recv.at[j - 1, k],
+                src_ref=piece(place if k else own_weights, c),
+                dst_ref=piece(place, c),
+                send_sem=gx_send.at[j - 1, k, c],
+                recv_sem=gx_recv.at[j - 1, k, c],
                 device_id={"shard": shard_at(j)},
                 device_id_type=MESH,
             )
             copy.start()
-            gx_copies[j, k] = copy
+            gx_copies[j, k, c] = copy
             sends.append(copy)
 
-    forward(0, own_weights)
-    gz_copies = {}
-    for k in order[:-1]:
-        copy = pltpu.make_async_remote_copy(
-            src_ref=own_weights,
-            dst_ref=weights.at[s, z],
-            send_sem=gz_send.at[k - 1],
-            recv_sem=gz_recv.at[k - 1],
-            device_id={"section": section_at(k)},
-            device_id_type=MESH,
-        )
-        copy.start()
-        gz_copies[k] = copy
-        sends.append(copy)
+    def spread(c):
+        for k in order[:-1]:
+            copy = pltpu.make_async_remote_copy(
+                src_ref=piece(own_weights, c),
+                dst_ref=piece(weights.at[s, z], c),
+                send_sem=gz_send.at[k - 1, c],
+                recv_sem=gz_recv.at[k - 1, c],
+                device_id={"section": section_at(k)},
+                device_id_type=MESH,
+            )
+            copy.start()
+            gz_copies[k, c] = copy
+            sends.append(copy)
+        forward(0, c)
+
+    for c in range(min(DEPTH, PIECES)):
+        spread(c)
     own = pltpu.make_async_copy(own_weights, weights.at[s, z], own_sem)
     own.start()
     stores = []
@@ -243,9 +254,12 @@
         copy = pltpu.make_async_copy(new_buf[i], new_states[i], store_sem.at[i])
         copy.start()
         stores.append(copy)
-    for k in reversed(order[:-1]):
-        gz_copies[k].wait_recv()
-        forward(k, weights.at[s, lax.rem(z - k + sections, sections)])
+    for c in range(PIECES):
+        for k in order[:-1]:
+            gz_copies[k, c].wait_recv()
+            forward(k, c)
+        if c + DEPTH < PIECES:
+            spread(c + DEPTH)
     own.wait()
     for copy in stores:
         copy.wait()
@@ -311,10 +325,10 @@
             dma((n_group,)),
             dma((tensors - 1,)),
             dma((tensors - 1,)),
-            dma((sections - 1,)),
-            dma((sections - 1,)),
-            dma((shards - 1, sections)),
-            dma((shards - 1, sections)),
+            dma((sections - 1, PIECES)),
+            dma((sections - 1, PIECES)),
+            dma((shards - 1, sections, PIECES)),
+            dma((shards - 1, sections, PIECES)),
         ]
     )
     results = pl.pallas_call(

time: 74.4 us -> 66 us (0.89); the launches traced: 73.1 us -> 65.9 us
  Pallas kernels: 72.4 us -> 65.2 us
    pallas_call x1, Pallas kernels: 70.7 us -> 63.5 us  [on_device(): pl.pallas_call(functools.partial(kernel, (shards, sections, tensors), row...]
where the time goes in v3:
time: 66 us; the launch traced here: 65.9 us
  Pallas kernels  65.2 us (99%)
  between operations  0.66 us (1%)
    pallas_call x1, Pallas kernels, on_device(): pl.pallas_call(functools.partial(kernel, (shards, sections, tensors), row...  63.5 us
    pallas_call x1, Pallas kernels, on_device(): pl.pallas_call(functools.partial(finish, rows), out_shape=[jax.ShapeDtype...  1.7 us

profile of v3, /device:TPU:0, one launch (start us, length us, event | category | flops | bytes accessed | tf_op | source)
XLA Modules:
  0.0 65.9 jit_solution(6659505542443102393)
XLA Ops:
  0.6 63.5 %shard_map.211 = (f32[128,512]{1,0:T(8,128)S(1)}, f32[64,512]{1,0:T(8,128)S(1)}, f32[16,512]{1,0:T(8,128)S(1)}, f32[128,512]{1,0:T(8,128)S(1)}, f32[64,512]{1,0:...) custom-call(bf16[2,2,4,128,512]{4,3,2,1,0:T(8,128)(2,1)} %bitcast.6,, ...), custom_call_target="tpu_custom_call" | custom-call | tf_op jit(solution)/shard_map/pallas_call | solution.py:334
  64.2 1.7 %shard_map.212 = (f32[128,512]{1,0:T(8,128)}, f32[64,512]{1,0:T(8,128)}, f32[16,512]{1,0:T(8,128)}, f32[128,512]{1,0:T(8,128)}, f32[64,512]{1,0:T(8,128)}, /*ind...) custom-call(f32[128,512]{1,0:T(8,128)S(1)} %get-tuple-element.34.ref, ...), custom_call_target="tpu_custom_call" | custom-call | tf_op jit(solution)/shard_map/pallas_call | solution.py:348
